TPU v7x, 512 devices: a whole 4x8x8 slice. The times are simulated.
512 devices in a mesh: prow: 16 (over y, core), pcol: 32 (over z, x).
Axes of the slice: x: 4, y: 8, z: 8, core: 2. Of those that a mesh axis runs over, the one named last changes fastest.
Arguments:
- matrix: bfloat16 [2, 16, 512, 2, 32, 512], P(None, 'prow', None, None, 'pcol'), may hold values from -6 to 6
- pivots: int32 [2, 512], replicated, may hold values from 0 to 16383, as said below
- lower_inverse: bfloat16 [2, 512, 512], replicated, as said below
- upper_inverse: bfloat16 [2, 512, 512], replicated, as said below
Outputs:
- factored: bfloat16 [2, 16, 512, 2, 32, 512], P(None, 'prow', None, None, 'pcol')
Inputs may be any that keep to these rules, and one draw needn't show every extreme that they name: Each row of pivots holds 512 distinct row indices; those of panel k are k * 512 or more. lower_inverse[k] is unit lower triangular. upper_inverse[k] is upper triangular with a positive diagonal.
All inputs are finite; a program needn't handle non-finite values.
Results may differ from a plain program's by a relative error of at most 0.0084.
Values may be sent and summed in bfloat16 or wider, within the bound.
A program may use at most 64 MiB of HBM per device.

v0:
```python
import jax
import jax.numpy as jnp
from jax import lax
from jax.sharding import PartitionSpec as P

PANELS = 2


def from_root(value, axis, root):
    mine = lax.axis_index(axis) == root
    return lax.psum(jnp.where(mine, value, jnp.zeros_like(value)), axis)


def pairing(sources, first_row, panel_width):
    top_ids = first_row + jnp.arange(panel_width, dtype=jnp.int32)
    chosen = jnp.any(sources[None, :] == top_ids[:, None], axis=1)
    leftover = jnp.logical_not(chosen)
    left_rank = jnp.cumsum(leftover.astype(jnp.int32)) - 1
    vacated = sources >= first_row + panel_width
    vac_rank = jnp.cumsum(vacated.astype(jnp.int32)) - 1
    match_table = leftover[None, :] & (left_rank[None, :] == vac_rank[:, None])
    receive = jnp.sum(jnp.where(match_table, top_ids[None, :], 0), axis=1)
    return (receive, vacated)


def per_device(matrix, pivots, lower_inverse, upper_inverse):
    shape_in = matrix.shape
    row_blocks = shape_in[0]
    block_size = shape_in[2]
    col_blocks = shape_in[3]
    local_tile = matrix.reshape(row_blocks * block_size, col_blocks * block_size)
    prow_count = lax.axis_size("prow")
    pcol_count = lax.axis_size("pcol")
    prow_index = lax.axis_index("prow")
    pcol_index = lax.axis_index("pcol")
    local_rows = jnp.arange(row_blocks * block_size, dtype=jnp.int32)
    rows_global = (
        local_rows // block_size * prow_count + prow_index
    ) * block_size + local_rows % block_size
    local_cols = jnp.arange(col_blocks * block_size, dtype=jnp.int32)
    cols_global = (
        local_cols // block_size * pcol_count + pcol_index
    ) * block_size + local_cols % block_size
    for step_index in range(PANELS):
        first_row = step_index * block_size
        past_row = first_row + block_size
        sources = pivots[step_index]
        receive, vacated = pairing(sources, first_row, block_size)
        src_block = sources // block_size
        owner_row = src_block % prow_count
        src_local = src_block // prow_count * block_size + sources % block_size
        owned_row = owner_row == prow_index
        picked = jnp.take(local_tile, jnp.where(owned_row, src_local, 0), axis=0)
        contrib = jnp.where(owned_row[:, None], picked, jnp.zeros_like(picked))
        diag_row = step_index % prow_count
        diag_local = step_index // prow_count
        own_top = local_tile[diag_local * block_size : (diag_local + 1) * block_size]
        old_top = from_root(own_top, "prow", diag_row)
        hit_table = (rows_global[:, None] == sources[None, :]) & vacated[None, :]
        hit_rows = jnp.any(hit_table, axis=1)
        giver_row = jnp.sum(jnp.where(hit_table, receive[None, :] - first_row, 0), axis=1)
        local_tile = jnp.where(hit_rows[:, None], jnp.take(old_top, giver_row, axis=0), local_tile)
        cols_right = cols_global >= past_row
        top_rows = lax.psum(contrib, "prow").astype(jnp.float32).astype(jnp.bfloat16)
        upper_rows = jnp.dot(
            lower_inverse[step_index], top_rows, preferred_element_type=jnp.float32
        ).astype(jnp.bfloat16)
        row_block = jnp.where(cols_right[None, :], upper_rows, top_rows)
        update = jnp.where(cols_right[None, :], row_block, jnp.zeros_like(row_block))
        root_col = step_index % pcol_count
        panel_local = step_index // pcol_count
        below_rows = rows_global >= past_row
        panel_raw = local_tile[:, panel_local * block_size : (panel_local + 1) * block_size]
        is_root = pcol_index == root_col

        def compute():
            product = jnp.dot(
                panel_raw, upper_inverse[step_index], preferred_element_type=jnp.float32
            ).astype(jnp.bfloat16)
            return jnp.where(below_rows[:, None], product, jnp.zeros_like(product))

        def nothing():
            return jnp.zeros_like(panel_raw)

        factor = from_root(lax.cond(is_root, compute, nothing), "pcol", root_col)
        local_tile = (
            local_tile.astype(jnp.float32)
            - jnp.dot(factor, update, preferred_element_type=jnp.float32)
        ).astype(jnp.bfloat16)
        updated_slab = local_tile[:, panel_local * block_size : (panel_local + 1) * block_size]
        stored = jnp.where(below_rows[:, None] & is_root, factor, updated_slab)
        local_tile = local_tile.at[
            :, panel_local * block_size : (panel_local + 1) * block_size
        ].set(stored)
        is_diag = prow_index == diag_row
        current = local_tile[diag_local * block_size : (diag_local + 1) * block_size]
        local_tile = local_tile.at[diag_local * block_size : (diag_local + 1) * block_size].set(
            jnp.where(is_diag, row_block, current)
        )
    return local_tile.reshape(shape_in)


def solution(mesh):
    return jax.shard_map(
        per_device,
        mesh=mesh,
        in_specs=(P(None, "prow", None, None, "pcol", None), P(), P(), P()),
        out_specs=P(None, "prow", None, None, "pcol", None),
        check_vma=False,
    )
```

profile of v0, /device:TPU:8, one launch (start us, length us, event | category | flops | bytes accessed | tf_op | source)
XLA Modules:
  0.0 652.1 jit_solution(6534921439675607615)
XLA Ops:
  7.3 2.1 copy.57
  9.5 2.1 gather_fusion
  11.6 1.3 copy.37
  12.9 2.2 broadcast_select_fusion
  17.8 2.6 copy.52
  25.4 115.3 %all-reduce.13.cloned.1.call-done = (bf16[512,1024]{1,0:T(8,128)(2,1)}, bf16[512,1024]{0,1:T(8,128)(2,1)}) async-done(((bf16[512,1024]{1,0:T(8,128)(2,1)}, bf16[512,1024]{0,1:T(8,128)(2,1)}), (bf16[512,1024]{1,0:T(8,128)(2,1)}, bf16[512,1024]{0,1:T(8,128)(2,1)})) %all-reduce.13.cloned.1.call-update) | async-done | bytes 2097168 | tf_op jit(solution)/shard_map/psum | solution.py:11
  140.7 6.3 gather_fusion.1
  147.1 2.6 copy.38
  149.7 2.5 select_select_fusion.1
  152.1 7.0 %conditional.2 = (bf16[1024,512]{0,1:T(8,128)(2,1)S(1)}) conditional(s32[]{:T(128)} %convert_element_type.75, () %tuple.35, (pred[1024]{0:T(1024)(128)(4,1)S(1)}, bf16[2,512,512]{2,1,0:T(8,128)(2,1)}, bf16[1024,1024]{0,1:T(8,128)(2,1)S(1)}) %tuple.36), branch_computations={%region_11.14_spmd, %region_12.15_spmd} | conditional | flops 537919488 | bytes 13108260 | solution.py:85
  152.1 2.6 copy.39
  154.7 2.9 fusion
  157.6 1.5 copy.54
  161.1 2.4 fusion.11
  163.6 153.4 %all-reduce.7.cloned.1.call-done = bf16[1024,512]{0,1:T(8,128)(2,1)} async-done(((bf16[1024,512]{0,1:T(8,128)(2,1)}), bf16[1024,512]{0,1:T(8,128)(2,1)}) %all-reduce.7.cloned.1.call-update) | async-done | bytes 1048592 | tf_op jit(solution)/shard_map/psum | solution.py:11
  317.0 2.6 subtract_convert_fusion.1
  320.8 1.7 broadcast_select_fusion.3
  322.5 1.3 copy-done
  323.9 2.9 copy.46
  326.7 2.1 gather_fusion.3
  330.6 115.7 %all-reduce.11.cloned.1.call-done = (bf16[512,1024]{0,1:T(8,128)(2,1)}, bf16[512,1024]{0,1:T(8,128)(2,1)}) async-done(((bf16[512,1024]{0,1:T(8,128)(2,1)}, bf16[512,1024]{0,1:T(8,128)(2,1)}), (bf16[512,1024]{0,1:T(8,128)(2,1)}, bf16[512,1024]{0,1:T(8,128)(2,1)})) %all-reduce.11.cloned.1.call-update) | async-done | bytes 2097168 | tf_op jit(solution)/shard_map/psum | solution.py:11
  446.3 1.5 copy.42
  447.8 5.4 gather_fusion.2
  453.1 4.1 copy.43
  457.2 3.1 select_select_fusion
  461.7 2.6 fusion.13
  464.3 161.0 %all-reduce.9.cloned.1.call-done = bf16[1024,512]{0,1:T(8,128)(2,1)} async-done(((bf16[1024,512]{0,1:T(8,128)(2,1)}), bf16[1024,512]{0,1:T(8,128)(2,1)}) %all-reduce.9.cloned.1.call-update) | async-done | bytes 1048592 | tf_op jit(solution)/shard_map/psum | solution.py:11
  625.3 3.9 subtract_convert_fusion
  629.2 3.3 fusion.15
  632.5 2.5 fusion.16
  635.0 3.3 reshape.401
  638.3 7.3 %copy.49 = bf16[2,1,512,2,1,512]{5,3,4,2,1,0:T(2,128)(2,1)} copy(bf16[2,1,512,2,1,512]{2,0,5,3,4,1:T(2,128)(2,1)S(1)} %reshape.401) | data formatting | bytes 4194304 | tf_op jit(solution)/shard_map/reshape | solution.py:100
  (76 shorter events, 14.8 us)
Async XLA Ops:
  6.5 134.2 %all-reduce.13.cloned.1.call-start = ((), (), s32[]{:S(2)}) async-start(), calls=%async_computation.3 | async-start | bytes 4194304 | tf_op jit(solution)/shard_map/psum | solution.py:11
  12.9 3.4 copy-start.3
  16.3 1.2 copy-start.6
  17.5 299.5 %all-reduce.7.cloned.1.call-start = ((), (), s32[]{:S(2)}) async-start(), calls=%async_computation | async-start | bytes 2097152 | tf_op jit(solution)/shard_map/psum | solution.py:11
  152.1 2.6 copy-start.7
  160.2 286.1 %all-reduce.11.cloned.1.call-start = ((), (), s32[]{:S(2)}) async-start(), calls=%async_computation.2 | async-start | bytes 4194304 | tf_op jit(solution)/shard_map/psum | solution.py:11
  317.0 2.6 copy-start.4
  322.5 1.3 copy-start
  330.5 294.8 %all-reduce.9.cloned.1.call-start = ((), (), s32[]{:S(2)}) async-start(), calls=%async_computation.1 | async-start | bytes 2097152 | tf_op jit(solution)/shard_map/psum | solution.py:11
  453.1 4.1 copy-start.1
  461.6 163.7 %copy-start.2 = (bf16[1024,1024]{0,1:T(8,128)(2,1)S(1)}, bf16[1024,1024]{0,1:T(8,128)(2,1)}, u32[]{:S(2)}) copy-start(bf16[1024,1024]{0,1:T(8,128)(2,1)} %select_select_fusion) | copy-start | bytes 6291460
  625.3 3.9 copy-start.5
Sparse Core Ops, SparseCore 0:
  17.6 123.0 all-reduce.12
  160.3 156.6 all-reduce.6
  330.6 115.6 all-reduce.10
  461.8 163.4 all-reduce.8
where the time goes:
time: 653 us; the launch traced here: 652 us
  waiting for transfers between devices  546 us (84%)
  local copies, waits for them, and re-layouts  52.3 us (8%)
  other arithmetic  26 us (4%)
  matrix products  14.5 us (2%)
  between operations  13.4 us (2%)
    psum x4, waiting for transfers between devices, from_root(): return lax.psum(jnp.where(mine, value, jnp.zeros_like(value)), axis)  545 us
    gather x4, local copies, waits for them, and re-layouts, per_device(): jnp.take(old_top, giver_row, axis=0)  18.4 us
  transfers between devices with their start and end apart: 4, of which 4 were waited for; matrix products, arithmetic and copies ran while one was open for 2% of the time, Pallas kernels for 0%

commit v1 on v0

--- a/solution.py
+++ b/solution.py
@@ -6,9 +6,15 @@
 PANELS = 2
 
 
+def summed_here(x, axis):
+    parts = lax.all_gather(x, axis, axis=0, tiled=False)
+    total = parts.sum(axis=0)
+    return total
+
+
 def from_root(value, axis, root):
     mine = lax.axis_index(axis) == root
-    return lax.psum(jnp.where(mine, value, jnp.zeros_like(value)), axis)
+    return summed_here(jnp.where(mine, value, jnp.zeros_like(value)), axis)
 
 
 def pairing(sources, first_row, panel_width):

time: 653 us -> 995 us (1.52)
  the two profiles are of different devices: /device:TPU:8 before, /device:TPU:1 now
where the time goes in v1:
time: 995 us; the launch traced here: 994 us
  waiting for transfers between devices  835 us (84%)
  other arithmetic  70.2 us (7%)
  local copies, waits for them, and re-layouts  57.7 us (6%)
  matrix products  16.9 us (2%)
  between operations  13.7 us (1%)
    all_gather x4, waiting for transfers between devices, summed_here(): parts = lax.all_gather(x, axis, axis=0, tiled=False)  656 us
    psum x2, waiting for transfers between devices, per_device(): lax.psum(contrib, 'prow').astype(jnp.float32).astype(jnp.bfloat16)  179 us
    reduce_sum x4, other arithmetic, summed_here(): total = parts.sum(axis=0)  40.4 us
  transfers between devices with their start and end apart: 6, of which 6 were waited for; matrix products, arithmetic and copies ran while one was open for 9% of the time, Pallas kernels for 0%

profile of v1, /device:TPU:1, one launch (start us, length us, event | category | flops | bytes accessed | tf_op | source)
XLA Modules:
  0.0 994.0 jit_solution(323099062400877377)
XLA Ops:
  15.9 2.3 select_select_fusion.5
  23.6 2.6 copy.61
  26.2 87.8 %all-gather.8.cloned.1.call-done = bf16[16,512,1024]{2,1,0:T(8,128)(2,1)} async-done(((bf16[1,512,1024]{2,1,0:T(8,128)(2,1)}), bf16[16,512,1024]{2,1,0:T(8,128)(2,1)}) %all-gather.8.cloned.1.call-update) | async-done | bytes 16777232 | tf_op jit(solution)/shard_map/all_gather | solution.py:10
  114.0 9.3 reduce_sum.84
  123.3 4.1 gather_fusion.1
  127.4 2.6 copy.47
  130.0 2.5 select_select_fusion.1
  132.4 4.6 conditional.2
  132.5 2.6 copy.48
  139.1 92.5 %all-reduce.3.cloned.1.call-done = bf16[512,1024]{0,1:T(8,128)(2,1)} async-done(((bf16[512,1024]{0,1:T(8,128)(2,1)}), bf16[512,1024]{0,1:T(8,128)(2,1)}) %all-reduce.3.cloned.1.call-update) | async-done | bytes 1048592 | tf_op jit(solution)/shard_map/psum | solution.py:70
  231.6 3.5 fusion.11
  235.0 240.3 %all-gather.10.cloned.1.call-done = bf16[32768,512]{1,0:T(8,128)(2,1)} async-done(((bf16[1024,512]{1,0:T(8,128)(2,1)}), bf16[32768,512]{1,0:T(8,128)(2,1)}) %all-gather.10.cloned.1.call-update) | async-done | bytes 33554448 | tf_op jit(solution)/shard_map/all_gather | solution.py:10
  475.4 11.4 %reduce_sum.87 = bf16[1024,512]{1,0:T(8,128)(2,1)S(1)} reduce(bf16[32,1024,512]{2,1,0:T(8,128)(2,1)} %bitcast.57, bf16[]{:T(256)} %constant.279.clone.1), dimensions={0}, to_apply=%region_13.16 | reduce | flops 16252928 | bytes 34603008 | tf_op jit(solution)/shard_map/reduce_sum | solution.py:11
  488.1 4.0 subtract_convert_fusion.1
  492.1 3.3 fusion.14
  495.4 2.9 broadcast_select_fusion.3
  498.4 2.9 copy.54
  505.1 88.4 %all-gather.12.cloned.1.call-done = bf16[8192,1024]{0,1:T(8,128)(2,1)} async-done(((bf16[512,1024]{0,1:T(8,128)(2,1)}), bf16[8192,1024]{0,1:T(8,128)(2,1)}) %all-gather.12.cloned.1.call-update) | async-done | bytes 16777232 | tf_op jit(solution)/shard_map/all_gather | solution.py:10
  593.5 12.1 %copy.63 = bf16[128,8,16,512]{3,2,1,0:T(8,128)(2,1)S(1)} copy(bf16[128,8,16,512]{3,1,2,0:T(8,128)(2,1)} %bitcast.59) | data formatting | bytes 33554432
  605.6 8.2 bitcast_reduce_fusion
  614.4 4.1 gather_fusion.2
  618.4 2.6 copy.52
  621.0 2.5 select_select_fusion
  624.9 86.0 %all-reduce.5.cloned.1.call-done = bf16[512,1024]{0,1:T(8,128)(2,1)} async-done(((bf16[512,1024]{0,1:T(8,128)(2,1)}), bf16[512,1024]{0,1:T(8,128)(2,1)}) %all-reduce.5.cloned.1.call-update) | async-done | bytes 1048592 | tf_op jit(solution)/shard_map/psum | solution.py:70
  710.9 3.4 fusion.13
  714.4 239.7 %all-gather.14.cloned.1.call-done = bf16[32768,512]{1,0:T(8,128)(2,1)} async-done(((bf16[1024,512]{1,0:T(8,128)(2,1)}), bf16[32768,512]{1,0:T(8,128)(2,1)}) %all-gather.14.cloned.1.call-update) | async-done | bytes 33554448 | tf_op jit(solution)/shard_map/all_gather | solution.py:10
  954.1 11.4 %reduce_sum.91 = bf16[1024,512]{1,0:T(8,128)(2,1)S(1)} reduce(bf16[32,1024,512]{2,1,0:T(8,128)(2,1)} %bitcast.58, bf16[]{:T(256)} %constant.279.clone.1), dimensions={0}, to_apply=%region_25.28 | reduce | flops 16252928 | bytes 34603008 | tf_op jit(solution)/shard_map/reduce_sum | solution.py:11
  966.9 3.9 subtract_convert_fusion
  970.8 3.3 fusion.15
  974.1 2.5 fusion.16
  976.6 3.3 reshape.411
  979.9 7.3 copy.58
  (82 shorter events, 27.2 us)
Async XLA Ops:
  6.5 107.5 %all-gather.8.cloned.1.call-start = ((), (), s32[]{:S(2)}) async-start(), calls=%async_computation.1 | async-start | bytes 17825792 | tf_op jit(solution)/shard_map/all_gather | solution.py:10
  10.2 221.4 %all-reduce.3.cloned.1.call-start = ((), (), s32[]{:S(2)}) async-start(), calls=%async_computation | async-start | bytes 2097152 | tf_op jit(solution)/shard_map/psum | solution.py:70
  10.2 2.2 copy-start.4
  18.3 457.1 %all-gather.10.cloned.1.call-start = ((), (), s32[]{:S(2)}) async-start(), calls=%async_computation.3 | async-start | bytes 34603008 | tf_op jit(solution)/shard_map/all_gather | solution.py:10
  138.2 455.4 %all-gather.12.cloned.1.call-start = ((), (), s32[]{:S(2)}) async-start(), calls=%async_computation.4 | async-start | bytes 17825792 | tf_op jit(solution)/shard_map/all_gather | solution.py:10
  488.1 4.0 copy-start.1
  492.1 3.3 copy-start.2
  498.3 212.6 %all-reduce.5.cloned.1.call-start = ((), (), s32[]{:S(2)}) async-start(), calls=%async_computation.2 | async-start | bytes 2097152 | tf_op jit(solution)/shard_map/psum | solution.py:70
  505.0 449.1 %all-gather.14.cloned.1.call-start = ((), (), s32[]{:S(2)}) async-start(), calls=%async_computation.5 | async-start | bytes 34603008 | tf_op jit(solution)/shard_map/all_gather | solution.py:10
  966.9 3.9 copy-start
  970.8 3.3 copy-start.3
Sparse Core Ops, SparseCore 0:
  10.3 103.6 all-gather.7
  116.3 115.2 all-reduce.2
  235.2 240.0 all-gather.9
  498.4 95.0 all-gather.11
  595.8 115.1 all-reduce.4
  714.0 240.0 all-gather.13
